TPU v7x, 32 devices: a whole 2x2x4 slice. The times are simulated.
32 devices in a mesh: dp: 2 (over x), expert: 8 (over z, y), tensor: 2 (over core).
Axes of the slice: x: 2, y: 2, z: 4, core: 2. Of those that a mesh axis runs over, the one named last changes fastest.
Arguments:
- activations: bfloat16 [4096, 1536], P(('dp', 'expert', 'tensor')), may hold values from -6 to 6
- segments: int32 [16, 256], P(('dp', 'expert')), may hold values from 0 to 3, never falling along the last dimension, each value on 1 to 128 neighbouring positions
- routes: int32 [4096, 8], P(('dp', 'expert', 'tensor')), may hold values from 0 to 15, all different within a row; in each aligned block of 128 rows (0 to 127, 128 to 255, ...) at most 128 rows name the same one
- route_weights: float32 [4096, 8], P(('dp', 'expert', 'tensor')), may hold values from 0.03 to 0.3
- norm_attn_gain: float32 [1536], replicated, may hold values from 0.5 to 1.5
- norm_ffn_gain: float32 [1536], replicated, may hold values from 0.5 to 1.5
- query_weight: bfloat16 [1536, 1536], P(None, 'tensor'), may hold values from -0.15625 to 0.15625
- key_matrix: bfloat16 [1536, 512], P(None, 'tensor'), may hold values from -0.15625 to 0.15625
- value_matrix: bfloat16 [1536, 512], P(None, 'tensor'), may hold values from -0.15625 to 0.15625
- output_projection_weight: bfloat16 [1536, 1536], P('tensor'), may hold values from -0.625 to 0.625
- expert_gate: bfloat16 [16, 1536, 512], P('expert', None, 'tensor'), may hold values from -0.15625 to 0.15625
- expert_up: bfloat16 [16, 1536, 512], P('expert', None, 'tensor'), may hold values from -0.15625 to 0.15625
- expert_down: bfloat16 [16, 512, 1536], P('expert', 'tensor'), may hold values from -0.5 to 0.5
- grad_output: bfloat16 [4096, 1536], P(('dp', 'expert', 'tensor')), may hold values from -6 to 6
Outputs:
- block_out: bfloat16 [4096, 1536], P(('dp', 'expert', 'tensor'))
- grad_input: float32 [4096, 1536], P(('dp', 'expert', 'tensor'))
- grad_norm_attn: float32 [1536], replicated
- grad_norm_ffn: float32 [1536], replicated
- grad_query: float32 [1536, 1536], P(None, 'tensor')
- grad_key: float32 [1536, 512], P(None, 'tensor')
- grad_value: float32 [1536, 512], P(None, 'tensor')
- grad_mixer: float32 [1536, 1536], P('tensor')
- grad_expert_gate: float32 [16, 1536, 512], P('expert', None, 'tensor')
- grad_expert_up: float32 [16, 1536, 512], P('expert', None, 'tensor')
- grad_expert_down: float32 [16, 512, 1536], P('expert', 'tensor')
Inputs may be any that keep to these rules, and one draw needn't show every extreme that they name: `routes`: each row names 8 different experts; in the rows of one device (aligned blocks of 128 rows) no expert is named more than 128 times, and one is named exactly 128 times in some block. `segments`: each sequence's numbers never fall; 4 documents of 1 to 128 positions, one of exactly 128.
All inputs are finite; a program needn't handle non-finite values.
Results may differ from a plain program's by a relative error of at most 0.01.
Values may be sent and summed in bfloat16 or wider, within the bound.
No kernel may reach another device: no remote copies, remote signals or barrier semaphores. Data moves between devices by JAX's collectives and lax.ppermute only.
A program may use at most 320 MiB of HBM per device.

v0:
```python
import jax
import jax.numpy as jnp
from jax import lax
from jax.sharding import PartitionSpec as P

HEAD_DIM = 64
EPS = 1e-05
ATTN_SCALE = 0.015625
THETA = 10000.0
NEG_FILL = -1e30
F32 = jnp.float32
BF16 = jnp.bfloat16


def swap(values):
    return lax.ppermute(values, "tensor", [(0, 1), (1, 0)])


def norm_forward(values, gain_vector):
    inv_scale = lax.rsqrt(jnp.mean(values * values, axis=-1, keepdims=True) + EPS)
    return (values * inv_scale * gain_vector, inv_scale)


def norm_backward(values, inv_scale, gain_vector, upstream):
    weighted = upstream * gain_vector
    inner = jnp.mean(weighted * values, axis=-1, keepdims=True)
    value_gradient = inv_scale * weighted - values * (inv_scale * inv_scale * inv_scale) * inner
    grad_gain = jnp.sum(upstream * values * inv_scale, axis=0)
    return (value_gradient, grad_gain)


def rope_tables(position):
    frequency = THETA ** (-jnp.arange(HEAD_DIM // 2, dtype=F32) * 2.0 / HEAD_DIM)
    angle_table = position.astype(F32)[:, None] * frequency[None, :]
    return (jnp.cos(angle_table)[:, None, :], jnp.sin(angle_table)[:, None, :])


def rotate(field_in, cosine, sine):
    first, second = jnp.split(field_in, 2, axis=-1)
    return jnp.concatenate(
        [first * cosine - second * sine, second * cosine + first * sine], axis=-1
    )


def dot(spec, left, right):
    return jnp.einsum(spec, left, right, preferred_element_type=F32)


def body(
    activations,
    segments,
    routes,
    route_weights,
    norm_attn_gain,
    norm_ffn_gain,
    query_weight,
    key_matrix,
    value_matrix,
    output_projection_weight,
    expert_gate,
    expert_up,
    expert_down,
    grad_output,
):
    tensor_rank = lax.axis_index("tensor")
    rows, width = activations.shape
    experts_here = expert_gate.shape[0]
    expert_count = experts_here * lax.axis_size("expert")
    length = segments.shape[1]
    heads_q = query_weight.shape[1] // HEAD_DIM
    heads_kv = key_matrix.shape[1] // HEAD_DIM
    group = heads_q // heads_kv
    position = (jnp.arange(length, dtype=jnp.int32) + tensor_rank * rows) % length
    seg_ids = jnp.where(tensor_rank == 0, segments[0], jnp.roll(segments[0], rows))
    cosine, sine = rope_tables(position)
    allowed = (position[None, :] <= position[:, None]) & (seg_ids[None, :] == seg_ids[:, None])
    gate = jnp.concatenate([expert_gate, swap(expert_gate)], axis=2)
    up = jnp.concatenate([expert_up, swap(expert_up)], axis=2)
    down = jnp.concatenate([expert_down, swap(expert_down)], axis=1)
    upstream_all = lax.all_gather(grad_output, "expert", axis=0, tiled=True)
    named = routes[:, :, None] == jnp.arange(expert_count, dtype=jnp.int32)
    weight_table = jnp.sum(jnp.where(named, route_weights[:, :, None], 0.0), axis=1)
    weights_all = lax.all_gather(weight_table, "expert", axis=0, tiled=True)
    first_expert = lax.axis_index("expert") * experts_here
    weights_here = lax.dynamic_slice_in_dim(weights_all, first_expert, experts_here, 1).T
    x_in = jnp.concatenate([activations, swap(activations)], axis=0).astype(F32)
    normed_one, scale_one = norm_forward(x_in, norm_attn_gain)
    hidden_first = normed_one.astype(BF16)
    queries = dot("td,da->ta", hidden_first, query_weight).reshape(length, heads_q, HEAD_DIM)
    queries = rotate(queries, cosine, sine).astype(BF16).reshape(length, heads_kv, group, HEAD_DIM)
    keys = dot("td,da->ta", hidden_first, key_matrix).reshape(length, heads_kv, HEAD_DIM)
    keys = rotate(keys, cosine, sine).astype(BF16)
    value_rows = dot("td,da->ta", hidden_first, value_matrix).astype(BF16)
    value_rows = value_rows.reshape(length, heads_kv, HEAD_DIM)
    scores = jnp.where(allowed, dot("qhgd,khd->hgqk", queries, keys) * ATTN_SCALE, NEG_FILL)
    top_score = jnp.max(scores, axis=-1, keepdims=True)
    log_total = top_score + jnp.log(jnp.sum(jnp.exp(scores - top_score), axis=-1, keepdims=True))
    mixed = dot("hgqk,khd->qhgd", jnp.exp(scores - log_total).astype(BF16), value_rows).astype(BF16)
    mixed_flat = mixed.reshape(length, heads_q * HEAD_DIM)
    attn_part = dot("ta,ad->td", mixed_flat, output_projection_weight)
    residual = x_in[:rows] + attn_part[:rows] + swap(attn_part[rows:])
    normed_two, scale_two = norm_forward(residual, norm_ffn_gain)
    tokens_in = lax.all_gather(normed_two.astype(BF16), "expert", axis=0, tiled=True)
    pre_gate = dot("td,edf->etf", tokens_in, gate)
    pre_up = dot("td,edf->etf", tokens_in, up)
    gate_sigmoid = jax.nn.sigmoid(pre_gate)
    activated = (pre_gate * gate_sigmoid * pre_up).astype(BF16)
    expert_out = dot("etf,efd->etd", activated, down).astype(BF16)
    mix_part = jnp.sum(weights_here[:, :, None] * expert_out.astype(F32), axis=0).astype(BF16)
    grad_rows = (weights_here[:, :, None] * upstream_all.astype(F32)[None]).astype(BF16)
    grad_act = dot("etd,efd->etf", grad_rows, down)
    grad_pre_gate = (
        grad_act * pre_up * gate_sigmoid * (1.0 + pre_gate * (1.0 - gate_sigmoid))
    ).astype(BF16)
    grad_pre_up = (grad_act * pre_gate * gate_sigmoid).astype(BF16)
    grad_in = dot("etf,edf->etd", grad_pre_gate, gate) + dot("etf,edf->etd", grad_pre_up, up)
    grad_part = jnp.sum(weights_here[:, :, None] * grad_in, axis=0).astype(BF16)
    grad_h_own = lax.psum_scatter(grad_part, "expert", scatter_dimension=0, tiled=True)
    expert_mix = lax.psum_scatter(mix_part, "expert", scatter_dimension=0, tiled=True)
    block_out = (residual + expert_mix.astype(F32)).astype(BF16)

    def expert_sum(whole, axis):
        own, other = jnp.split(whole, 2, axis=axis)
        half = own + swap(other.astype(BF16)).astype(F32)
        return lax.psum(half.astype(BF16), "dp").astype(F32)

    gate_sum = expert_sum(dot("td,etf->edf", tokens_in, grad_pre_gate), 2)
    up_sum = expert_sum(dot("td,etf->edf", tokens_in, grad_pre_up), 2)
    down_sum = expert_sum(dot("etf,etd->efd", activated, grad_rows), 1)
    upstream_own = grad_output.astype(F32)
    grad_norm_part, grad_ffn_gain = norm_backward(
        residual, scale_two, norm_ffn_gain, grad_h_own.astype(F32)
    )
    grad_resid = upstream_own + grad_norm_part
    resid_own = grad_resid.astype(BF16)
    resid_full = jnp.concatenate([resid_own, swap(resid_own)], axis=0)
    grad_mix_w = dot("sa,sb->ab", mixed_flat, resid_full)
    mixed_grad = dot("im,dm->id", resid_full, output_projection_weight).astype(BF16)
    mixed_grad = mixed_grad.reshape(length, heads_kv, group, HEAD_DIM)
    probs = jnp.exp(scores - log_total)
    row_delta = dot("qhgd,qhgd->hgq", mixed_grad, mixed)
    grad_soft = dot("qhgd,khd->hgqk", mixed_grad, value_rows)
    grad_scores = (probs * (grad_soft - row_delta[..., None]) * ATTN_SCALE).astype(BF16)
    grad_queries = dot("hgqk,khd->qhgd", grad_scores, keys)
    grad_keys = dot("hgqk,qhgd->khd", grad_scores, queries)
    grad_values = dot("hgqk,qhgd->khd", probs.astype(BF16), mixed_grad)
    grad_q_rows = rotate(grad_queries.reshape(length, heads_q, HEAD_DIM), cosine, -sine)
    grad_q_rows = grad_q_rows.astype(BF16).reshape(length, -1)
    grad_k_rows = rotate(grad_keys, cosine, -sine).astype(BF16).reshape(length, -1)
    grad_v_rows = grad_values.astype(BF16).reshape(length, -1)
    grad_q_w = dot("sd,sa->da", hidden_first, grad_q_rows)
    grad_k_w = dot("sd,sa->da", hidden_first, grad_k_rows)
    grad_v_w = dot("sd,sa->da", hidden_first, grad_v_rows)
    grad_h_part = (
        dot("sa,da->sd", grad_q_rows, query_weight)
        + dot("sa,da->sd", grad_k_rows, key_matrix)
        + dot("sa,da->sd", grad_v_rows, value_matrix)
    )
    grad_h_one = grad_h_part[:rows] + swap(grad_h_part[rows:])
    grad_x_part, grad_attn_gain = norm_backward(
        x_in[:rows], scale_one[:rows], norm_attn_gain, grad_h_one
    )
    grad_input = grad_resid + grad_x_part
    dense = [t.astype(BF16) for t in (grad_q_w, grad_k_w, grad_v_w, grad_mix_w)]
    dense = [t.astype(F32) for t in lax.psum(dense, ("dp", "expert"))]
    gains = lax.psum(jnp.stack([grad_attn_gain, grad_ffn_gain]), ("dp", "expert", "tensor"))
    return (block_out, grad_input, gains[0], gains[1], *dense, gate_sum, up_sum, down_sum)


def solution(mesh):
    tokens = P(("dp", "expert", "tensor"), None)
    whole = P()
    columns = P(None, "tensor")
    hidden_last = P("expert", None, "tensor")
    hidden_mid = P("expert", "tensor", None)
    mixer = P("tensor", None)
    return jax.shard_map(
        body,
        mesh=mesh,
        in_specs=(
            tokens,
            P(("dp", "expert"), None),
            tokens,
            tokens,
            whole,
            whole,
            columns,
            columns,
            columns,
            mixer,
            hidden_last,
            hidden_last,
            hidden_mid,
            tokens,
        ),
        out_specs=(
            tokens,
            tokens,
            whole,
            whole,
            columns,
            columns,
            columns,
            mixer,
            hidden_last,
            hidden_last,
            hidden_mid,
        ),
        check_vma=False,
    )
```

profile of v0, /device:TPU:0, one launch (start us, length us, event | category | flops | bytes accessed | tf_op | source)
XLA Modules:
  0.0 691.7 jit_solution(6405158610316332684)
XLA Ops:
  32.3 32.2 %all_gather.9 = f32[1024,16]{0,1:T(8,128)S(1)} all-gather(f32[128,16]{0,1:T(8,128)S(1)} %select_reduce_fusion), channel_id=1, replica_groups=mesh['dp'=2,'expert'=8,'tensor'=2] {'expert'}, dimensions={0}, use_global_device_ids=true | all-gather | bytes 73728 | tf_op jit(solution)/shard_map/all_gather | solution.py:83
  69.9 4.5 all-gather.5.cloned.1.call-done
  74.3 5.4 convert_element_type.165
  79.7 56.4 %all-gather.3.cloned.1.call-done = bf16[1024,1536]{1,0:T(8,128)(2,1)} async-done(((bf16[128,1536]{1,0:T(8,128)(2,1)}), bf16[1024,1536]{1,0:T(8,128)(2,1)}) %all-gather.3.cloned.1.call-update) | async-done | bytes 3145744 | tf_op jit(solution)/shard_map/all_gather | solution.py:103
  136.1 6.9 %fusion.24 = f32[2,512,1024]{2,1,0:T(8,128)S(1)} fusion(bf16[1024,1536]{1,0:T(8,128)(2,1)} %all-gather.3.cloned.1.call-done, bf16[2,1536,256]{1,2,0:T(8,128)(2,1)} %collective-permute-done.3, bf16[2,1536,256]{1,2,0:T(8,128)(2,1)} %copy.79), kind=kOutput, calls=%fused_computation.46 | convolution fusion | flops 3227516928 | bytes 10485760 | tf_op jit(solution)/shard_map/td,edf->etf/dot_general | solution.py:46
  143.1 6.5 fusion.26
  149.7 9.5 %fusion.9 = (bf16[2,1024,512]{1,2,0:T(8,128)(2,1)}, bf16[2,1024,512]{1,2,0:T(8,128)(2,1)}, bf16[2,1024,512]{1,2,0:T(8,128)(2,1)S(1)}) fusion(f32[2,512,1024]{2,1,0:T(8,128)S(1)} %fusion.24, f32[2,512,1024]{2,1,0:T(8,128)} %fusion.26, bf16[2,512,1536]{2,1,0:T(8,128)(2,1)} %constant_dynamic-update-slice_fusion, f32[1024,1536]{1,0:T(8,128)S(1)} %bitcast.160, ...), kind=kOutput, calls=%fused_computation.16 | convolution fusion | flops 3244294144 | bytes 24125440 | tf_op jit(solution)/shard_map/etd,efd->etf/dot_general | solution.py:46
  159.1 8.6 %fusion.30 = f32[2,1024,1536]{2,1,0:T(8,128)} fusion(bf16[2,1024,512]{1,2,0:T(8,128)(2,1)S(1)} %get-tuple-element.61, bf16[2,1536,256]{1,2,0:T(8,128)(2,1)} %collective-permute-done.3, bf16[2,1536,256]{1,2,0:T(8,128)(2,1)S(1)} %copy-done.11), kind=kOutput, calls=%fused_computation.59 | convolution fusion | flops 3227516928 | bytes 17825792 | tf_op jit(solution)/shard_map/etf,edf->etd/dot_general | solution.py:46
  167.7 13.0 %multiply_reduce_fusion = bf16[1024,1536]{1,0:T(8,128)(2,1)} fusion(f32[2,1024,1536]{2,1,0:T(8,128)} %fusion.30, f32[2,1024]{1,0:T(2,128)S(1)} %dynamic-slice_bitcast_fusion, bf16[2,1024,512]{1,2,0:T(8,128)(2,1)} %get-tuple-element.59, bf16[2,1536,256]{1,2,0:T(8,128)(2,1)} %collective-permute-done.2, bf16[2,1536,256]{1,2,0:T(8,128)(2,1)} %copy.77), kind=kOutput, calls=%fused_computation | convolution fusion | flops 3235381248 | bytes 20979712 | tf_op jit(solution)/shard_map/etf,edf->etd/dot_general | solution.py:46
  181.0 7.1 %fusion = f32[2,512,1536]{2,1,0:T(8,128)S(1)} fusion(bf16[2,1024,512]{1,2,0:T(8,128)(2,1)} %get-tuple-element.60, f32[1024,1536]{1,0:T(8,128)} %convert_element_type.165, f32[2,1024]{1,0:T(2,128)S(1)} %dynamic-slice_bitcast_fusion), kind=kOutput, calls=%fused_computation.3 | convolution fusion | flops 3227516928 | bytes 14688256 | tf_op jit(solution)/shard_map/etf,etd->efd/dot_general | solution.py:46
  190.0 3.4 convolution_bitcast_fusion.1
  195.0 3.4 convolution_bitcast_fusion
  203.8 8.9 %multiply_reduce_fusion.1 = bf16[1024,1536]{1,0:T(8,128)(2,1)} fusion(f32[2,1024]{1,0:T(2,128)S(1)} %dynamic-slice_bitcast_fusion, bf16[2,1024,512]{1,2,0:T(8,128)(2,1)} %get-tuple-element.60, bf16[2,512,1536]{2,1,0:T(8,128)(2,1)} %constant_dynamic-update-slice_fusion), kind=kOutput, calls=%fused_computation.2 | convolution fusion | flops 3232235520 | bytes 8396800 | tf_op jit(solution)/shard_map/etf,efd->etd/dot_general | solution.py:46
  212.9 41.2 %reduce-scatter.5.cloned.1.call-done = bf16[128,1536]{1,0:T(8,128)(2,1)} async-done(((bf16[1024,1536]{1,0:T(8,128)(2,1)}), bf16[128,1536]{1,0:T(8,128)(2,1)}) %reduce-scatter.5.cloned.1.call-update) | async-done | bytes 393232 | tf_op jit(solution)/shard_map/reduce_scatter | solution.py:118
  264.6 3.2 fusion.21
  287.1 88.6 %all-reduce.7.cloned.1.call-done = (bf16[2,1536,256]{1,2,0:T(8,128)(2,1)}, bf16[2,1536,256]{1,2,0:T(8,128)(2,1)}, bf16[2,256,1536]{2,1,0:T(8,128)(2,1)}) async-done(((bf16[2,1536,256]{1,2,0:T(8,128)(2,1)}, bf16[2,1536,256]{1,2,0:T(8,128)(2,1)}, bf16[2,256,1536]{2,1,0:T(8,128)(2,1)}), (bf16[2,1536,256]{1,2,0:T(8,128)(2,1)}, bf16[2,1536,256]{1,2,0:T(8,128)(2,1)}, ...) | async-done | bytes 4718608 | tf_op jit(solution)/shard_map/psum | solution.py:125
  375.8 3.1 copy.91
  378.8 3.1 copy.92
  381.9 3.6 convert_element_type.194
  388.2 40.9 %psum.56 = f32[2,1536]{1,0:T(2,128)} all-reduce(f32[2,1536]{1,0:T(2,128)} %pad_maximum_fusion.14), channel_id=1, replica_groups=mesh['dp'=2,'expert'=8,'tensor'=2] {'dp','expert','tensor'}, use_global_device_ids=true, to_apply=%region_13.14 | all-reduce | flops 3072 | bytes 24576 | tf_op jit(solution)/shard_map/psum | solution.py:166
  431.6 24.1 %reduce-scatter.3.cloned.1.call-done = bf16[128,1536]{1,0:T(8,128)(2,1)} async-done(((bf16[1024,1536]{1,0:T(8,128)(2,1)}), bf16[128,1536]{1,0:T(8,128)(2,1)}) %reduce-scatter.3.cloned.1.call-update) | async-done | bytes 393232 | tf_op jit(solution)/shard_map/reduce_scatter | solution.py:119
  455.7 3.3 subtract_add_fusion
  459.0 216.4 %all-reduce.5.cloned.1.call-done = (bf16[1536,768]{1,0:T(8,128)(2,1)}, bf16[1536,256]{1,0:T(8,128)(2,1)}, bf16[1536,256]{1,0:T(8,128)(2,1)}, bf16[768,1536]{1,0:T(8,128)(2,1)}) async-done(((bf16[1536,768]{1,0:T(8,128)(2,1)}, bf16[1536,256]{1,0:T(8,128)(2,1)}, bf16[1536,256]{1,0:T(8,128)(2,1)}, bf16[768,1536]{1,0:T(8,128)(2,1)}), (bf16[1536,768]{1,0:T(8,128)(2,1)}, bf16[1536,256]{1,0:T(8,128)(2,1)}, ...) | async-done | bytes 6291472 | tf_op jit(solution)/shard_map/psum | solution.py:165
  681.8 2.8 convert_element_type.185
  (239 shorter events, 80.4 us)
Async XLA Ops:
  7.2 13.7 %copy-start = (bf16[768,1536]{1,0:T(8,128)(2,1)S(1)}, bf16[768,1536]{1,0:T(8,128)(2,1)}, u32[]{:S(2)}) copy-start(bf16[768,1536]{1,0:T(8,128)(2,1)} %param.23) | copy-start | bytes 7077892
  7.2 67.1 %all-gather.5.cloned.1.call-start = ((), (), s32[]{:S(2)}) async-start(), calls=%async_computation.4 | async-start | bytes 3538944 | tf_op jit(solution)/shard_map/all_gather | solution.py:80
  8.0 128.2 %all-gather.3.cloned.1.call-start = ((), (), s32[]{:S(2)}) async-start(), calls=%async_computation.2 | async-start | bytes 3538944 | tf_op jit(solution)/shard_map/all_gather | solution.py:103
  8.0 3.7 collective-permute-start
  10.9 9.1 %copy-start.41 = (pred[256,256]{0,1:T(8,128)(4,1)}, pred[256,256]{0,1:T(8,128)(4,1)S(1)}, u32[]{:S(2)}) copy-start(pred[256,256]{0,1:T(8,128)(4,1)S(1)} %compare_and_fusion) | copy-start | bytes 196612
  11.7 10.1 %copy-start.15 = (bf16[128,1536]{1,0:T(8,128)(2,1)}, bf16[128,1536]{1,0:T(8,128)(2,1)S(1)}, u32[]{:S(2)}) copy-start(bf16[128,1536]{1,0:T(8,128)(2,1)S(1)} %collective-permute-done) | copy-start | bytes 1179652
  21.8 2.4 collective-permute-start.1
  26.4 227.7 %reduce-scatter.5.cloned.1.call-start = ((), (), s32[]{:S(2)}) async-start(), calls=%async_computation.5 | async-start | bytes 3538944 | tf_op jit(solution)/shard_map/reduce_scatter | solution.py:118
  26.4 40.8 %collective-permute-start.4 = (bf16[2,256,1536]{2,1,0:T(8,128)(2,1)}, bf16[2,256,1536]{2,1,0:T(8,128)(2,1)}, u32[]{:S(2)}, u32[]{:S(2)}) collective-permute-start(bf16[2,256,1536]{2,1,0:T(8,128)(2,1)} %param.26), channel_id=1, source_target_pairs={{0,1},{1,0},{2,3},{3,2},{4,5},{5,4},{6,7},{7,6},{8,9},{9,8},{10,11... | collective-permute-start | bytes 4718600 | tf_op jit(solution)/shard_map/ppermute | solution.py:16
  29.2 50.5 %collective-permute-start.3 = (bf16[2,1536,256]{1,2,0:T(8,128)(2,1)}, bf16[2,1536,256]{1,2,0:T(8,128)(2,1)}, u32[]{:S(2)}, u32[]{:S(2)}) collective-permute-start(bf16[2,1536,256]{1,2,0:T(8,128)(2,1)} %copy.79), channel_id=1, source_target_pairs={{0,1},{1,0},{2,3},{3,2},{4,5},{5,4},{6,7},{7,6},{8,9},{9,8},{10,11... | collective-permute-start | bytes 4718600 | tf_op jit(solution)/shard_map/ppermute | solution.py:16
  32.2 110.9 %collective-permute-start.2 = (bf16[2,1536,256]{1,2,0:T(8,128)(2,1)}, bf16[2,1536,256]{1,2,0:T(8,128)(2,1)}, u32[]{:S(2)}, u32[]{:S(2)}) collective-permute-start(bf16[2,1536,256]{1,2,0:T(8,128)(2,1)} %copy.77), channel_id=1, source_target_pairs={{0,1},{1,0},{2,3},{3,2},{4,5},{5,4},{6,7},{7,6},{8,9},{9,8},{10,11... | collective-permute-start | bytes 4718600 | tf_op jit(solution)/shard_map/ppermute | solution.py:16
  136.1 13.5 %slice-start = ((s8[6291456]{0:T(1024)(128)(4,1)}), s8[4194304]{0:T(1024)(128)(4,1)S(1)}, s32[]{:S(2)}) async-start(s8[6291456]{0:T(1024)(128)(4,1)} %bitcast.159), calls=%async_computation.8 | async-start | bytes 8388608
  149.6 9.5 %copy-start.11 = (bf16[2,1536,256]{1,2,0:T(8,128)(2,1)S(1)}, bf16[2,1536,256]{1,2,0:T(8,128)(2,1)}, u32[]{:S(2)}) copy-start(bf16[2,1536,256]{1,2,0:T(8,128)(2,1)} %copy.79) | copy-start | bytes 4718596
  180.8 195.0 %all-reduce.7.cloned.1.call-start = ((), (), s32[]{:S(2)}) async-start(), calls=%async_computation.7 | async-start | bytes 9437184 | tf_op jit(solution)/shard_map/psum | solution.py:125
  188.3 10.4 %collective-permute-start.9 = (bf16[2,256,1536]{2,1,0:T(8,128)(2,1)S(1)}, bf16[2,256,1536]{2,1,0:T(8,128)(2,1)S(1)}, u32[]{:S(2)}, u32[]{:S(2)}) collective-permute-start(bf16[2,256,1536]{2,1,0:T(8,128)(2,1)S(1)} %split.101), channel_id=1, source_target_pairs={{0,1},{1,0},{2,3},{3,2},{4,5},{5,4},{6,7},{7,6},{8,9},{9,8},{10,11... | collective-permute-start | bytes 4718600 | tf_op jit(solution)/shard_map/ppermute | solution.py:16
  193.6 6.7 collective-permute-start.7
  198.6 3.5 collective-permute-start.8
  203.7 252.0 %reduce-scatter.3.cloned.1.call-start = ((), (), s32[]{:S(2)}) async-start(), calls=%async_computation.3 | async-start | bytes 3538944 | tf_op jit(solution)/shard_map/reduce_scatter | solution.py:119
  212.6 41.5 %copy-start.52 = (f32[128]{0:T(128)S(1)}, f32[128]{0:T(128)}, u32[]{:S(2)}) copy-start(f32[128]{0:T(128)} %copy-done.51) | copy-start | bytes 1540
  212.6 43.3 %copy-start.56 = (f32[128]{0:T(128)S(1)}, f32[128]{0:T(128)}, u32[]{:S(2)}) copy-start(f32[128]{0:T(128)} %get-tuple-element.79) | copy-start | bytes 1540
  212.6 462.8 %all-reduce.5.cloned.1.call-start = ((), (), s32[]{:S(2)}) async-start(), calls=%async_computation.6 | async-start | bytes 12582912 | tf_op jit(solution)/shard_map/psum | solution.py:165
  257.4 1.8 collective-permute-start.5
  285.6 100.0 %collective-permute-start.6 = (f32[128,1536]{1,0:T(8,128)}, f32[128,1536]{1,0:T(8,128)}, u32[]{:S(2)}, u32[]{:S(2)}) collective-permute-start(f32[128,1536]{1,0:T(8,128)} %slice.53), channel_id=1, source_target_pairs={{0,1},{1,0},{2,3},{3,2},{4,5},{5,4},{6,7},{7,6},{8,9},{9,8},{10,11... | collective-permute-start | bytes 2359304 | tf_op jit(solution)/shard_map/ppermute | solution.py:16
  385.6 70.2 %copy-start.5 = (bf16[128,1536]{1,0:T(8,128)(2,1)S(1)}, bf16[128,1536]{1,0:T(8,128)(2,1)}, u32[]{:S(2)}) copy-start(bf16[128,1536]{1,0:T(8,128)(2,1)} %param.27) | copy-start | bytes 1179652
  (61 other events, 179.9 us)
Sparse Core Ops, SparseCore 0:
  10.2 64.0 all-gather.4
  77.1 58.9 all-gather.2
  180.9 73.1 reduce-scatter.4
  256.6 119.1 all-reduce.6
  380.2 75.4 reduce-scatter.2
  463.7 211.6 all-reduce.4
where the time goes:
time: 699 us; the launch traced here: 692 us
  waiting for transfers between devices  436 us (62%)
  matrix products  90.5 us (13%)
  blocking collectives  73.1 us (10%)
  other arithmetic  41.7 us (6%)
  local copies, waits for them, and re-layouts  32.8 us (5%)
  between operations  15.2 us (2%)
    psum x1, waiting for transfers between devices, body(): dense = [t.astype(F32) for t in lax.psum(dense, ('dp', 'expert'))]  216 us
    dot_general x27, matrix products, dot(): return jnp.einsum(spec, left, right, preferred_element_type=F32)  90.5 us
    psum x1, waiting for transfers between devices, expert_sum(): return lax.psum(half.astype(BF16), 'dp').astype(F32)  88.6 us
    all_gather x1, waiting for transfers between devices, body(): lax.all_gather(normed_two.astype(BF16), 'expert', axis=0, tiled=True)  56.4 us
    reduce_scatter x1, waiting for transfers between devices, body(): lax.psum_scatter(grad_part, 'expert', scatter_dimension=0, tiled=True)  41.2 us
    psum x1, blocking collectives, body(): lax.psum(jnp.stack([grad_attn_gain, grad_ffn_gain]), ('dp', 'expert', 'te...  40.9 us
    all_gather x1, blocking collectives, body(): weights_all = lax.all_gather(weight_table, 'expert', axis=0, tiled=True)  32.2 us
    reduce_scatter x1, waiting for transfers between devices, body(): lax.psum_scatter(mix_part, 'expert', scatter_dimension=0, tiled=True)  24.1 us
  transfers between devices with their start and end apart: 16, of which 8 were waited for; matrix products, arithmetic and copies ran while one was open for 16% of the time, Pallas kernels for 0%

commit v1 on v0

--- a/solution.py
+++ b/solution.py
@@ -10,6 +10,13 @@
 NEG_FILL = -1e30
 F32 = jnp.float32
 BF16 = jnp.bfloat16
+
+
+def balance_runs(inputs, row_data):
+    work_now = jnp.concatenate([inputs, row_data], 1)
+    mat_out = lax.all_gather(work_now, axis_name="expert", axis=0, tiled=True)
+    known = jnp.split(mat_out, [inputs.shape[1]], 1)
+    return known
 
 
 def swap(values):
@@ -77,10 +84,9 @@
     gate = jnp.concatenate([expert_gate, swap(expert_gate)], axis=2)
     up = jnp.concatenate([expert_up, swap(expert_up)], axis=2)
     down = jnp.concatenate([expert_down, swap(expert_down)], axis=1)
-    upstream_all = lax.all_gather(grad_output, "expert", axis=0, tiled=True)
     named = routes[:, :, None] == jnp.arange(expert_count, dtype=jnp.int32)
     weight_table = jnp.sum(jnp.where(named, route_weights[:, :, None], 0.0), axis=1)
-    weights_all = lax.all_gather(weight_table, "expert", axis=0, tiled=True)
+    upstream_all, weights_all = balance_runs(grad_output, weight_table)
     first_expert = lax.axis_index("expert") * experts_here
     weights_here = lax.dynamic_slice_in_dim(weights_all, first_expert, experts_here, 1).T
     x_in = jnp.concatenate([activations, swap(activations)], axis=0).astype(F32)

time: 699 us -> 753 us (1.077)
  waiting for transfers between devices: 436 us -> 512 us
  blocking collectives: 73.1 us -> 40.8 us
  local copies, waits for them, and re-layouts: 32.8 us -> 40.8 us
    all_gather x1, waiting for transfers between devices: 4.46 us -> 91.9 us  [balance_runs(): mat_out = lax.all_gather(work_now, axis_name='expert', axis=0, tiled=True)]
    all_gather x1 -> x0, blocking collectives: 32.2 us -> none  [body(): weights_all = lax.all_gather(weight_table, 'expert', axis=0, tiled=True)]
    all_gather x1, waiting for transfers between devices: 56.4 us -> 46.7 us  [body(): lax.all_gather(normed_two.astype(BF16), 'expert', axis=0, tiled=True)]
    unnamed x143 -> x139, local copies, waits for them, and re-layouts: 23.8 us -> 24.5 us
  transfers between devices with their start and end apart: 16 -> 16, of which waited for: 8 -> 8; matrix products, arithmetic and copies ran while one was open for 16% -> 14% of each run, Pallas kernels for 0% -> 0%
where the time goes in v1:
time: 753 us; the launch traced here: 747 us
  waiting for transfers between devices  512 us (68%)
  matrix products  94.4 us (13%)
  local copies, waits for them, and re-layouts  40.8 us (5%)
  blocking collectives  40.8 us (5%)
  other arithmetic  39.9 us (5%)
  between operations  15.4 us (2%)
    psum x1, waiting for transfers between devices, body(): dense = [t.astype(F32) for t in lax.psum(dense, ('dp', 'expert'))]  216 us
    dot_general x27, matrix products, dot(): return jnp.einsum(spec, left, right, preferred_element_type=F32)  94.4 us
    all_gather x1, waiting for transfers between devices, balance_runs(): mat_out = lax.all_gather(work_now, axis_name='expert', axis=0, tiled=True)  91.9 us
    psum x1, waiting for transfers between devices, expert_sum(): return lax.psum(half.astype(BF16), 'dp').astype(F32)  88.6 us
    all_gather x1, waiting for transfers between devices, body(): lax.all_gather(normed_two.astype(BF16), 'expert', axis=0, tiled=True)  46.7 us
    psum x1, blocking collectives, body(): lax.psum(jnp.stack([grad_attn_gain, grad_ffn_gain]), ('dp', 'expert', 'te...  40.8 us
    reduce_scatter x1, waiting for transfers between devices, body(): lax.psum_scatter(grad_part, 'expert', scatter_dimension=0, tiled=True)  40.6 us
    unnamed x139, local copies, waits for them, and re-layouts  24.5 us
  transfers between devices with their start and end apart: 16, of which 8 were waited for; matrix products, arithmetic and copies ran while one was open for 14% of the time, Pallas kernels for 0%

profile of v1, /device:TPU:0, one launch (start us, length us, event | category | flops | bytes accessed | tf_op | source)
XLA Modules:
  0.0 746.7 jit_solution(5621497385503620961)
XLA Ops:
  36.4 2.7 constant_dynamic-update-slice_fusion.1
  41.8 46.7 %all-gather.5.cloned.1.call-done = bf16[1024,1536]{1,0:T(8,128)(2,1)} async-done(((bf16[128,1536]{1,0:T(8,128)(2,1)}), bf16[1024,1536]{1,0:T(8,128)(2,1)}) %all-gather.5.cloned.1.call-update) | async-done | bytes 3145744 | tf_op jit(solution)/shard_map/all_gather | solution.py:109
  88.4 8.4 %fusion.24 = f32[2,512,1024]{2,1,0:T(8,128)} fusion(bf16[1024,1536]{1,0:T(8,128)(2,1)} %all-gather.5.cloned.1.call-done, bf16[2,1536,256]{1,2,0:T(8,128)(2,1)} %collective-permute-done.3, bf16[2,1536,256]{1,2,0:T(8,128)(2,1)} %copy.83), kind=kOutput, calls=%fused_computation.46 | convolution fusion | flops 3227516928 | bytes 10485760 | tf_op jit(solution)/shard_map/td,edf->etf/dot_general | solution.py:53
  96.9 6.6 fusion.26
  103.5 91.9 %all-gather.3.cloned.1.call-done = f32[1024,1552]{1,0:T(8,128)} async-done(((f32[128,1552]{1,0:T(8,128)}), f32[1024,1552]{1,0:T(8,128)}) %all-gather.3.cloned.1.call-update) | async-done | bytes 6357008 | tf_op jit(solution)/shard_map/all_gather | solution.py:17
  198.7 3.4 split.72
  202.7 11.6 %fusion.9 = (bf16[2,1024,512]{1,2,0:T(8,128)(2,1)}, bf16[2,1024,512]{1,2,0:T(8,128)(2,1)}, bf16[2,1024,512]{1,2,0:T(8,128)(2,1)S(1)}) fusion(f32[2,512,1024]{2,1,0:T(8,128)S(1)} %copy-done.66, f32[2,512,1024]{2,1,0:T(8,128)} %fusion.26, bf16[2,512,1536]{2,1,0:T(8,128)(2,1)} %constant_dynamic-update-slice_fusion, f32[1024,1536]{1,0:T(8,128)S(1)} %split.72, ...), kind=kOutput, calls=%fused_computation.16 | convolution fusion | flops 3244294144 | bytes 24125440 | tf_op jit(solution)/shard_map/etd,efd->etf/dot_general | solution.py:53
  214.4 8.7 %fusion.30 = f32[2,1024,1536]{2,1,0:T(8,128)} fusion(bf16[2,1024,512]{1,2,0:T(8,128)(2,1)S(1)} %get-tuple-element.61, bf16[2,1536,256]{1,2,0:T(8,128)(2,1)} %collective-permute-done.3, bf16[2,1536,256]{1,2,0:T(8,128)(2,1)S(1)} %copy-done.12), kind=kOutput, calls=%fused_computation.59 | convolution fusion | flops 3227516928 | bytes 17825792 | tf_op jit(solution)/shard_map/etf,edf->etd/dot_general | solution.py:53
  223.2 13.0 %multiply_reduce_fusion = bf16[1024,1536]{1,0:T(8,128)(2,1)} fusion(f32[2,1024,1536]{2,1,0:T(8,128)} %fusion.30, f32[2,1024]{1,0:T(2,128)S(1)} %copy.79, bf16[2,1024,512]{1,2,0:T(8,128)(2,1)} %get-tuple-element.59, bf16[2,1536,256]{1,2,0:T(8,128)(2,1)} %collective-permute-done.2, bf16[2,1536,256]{1,2,0:T(8,128)(2,1)} %copy.81), kind=kOutput, calls=%fused_computation | convolution fusion | flops 3235381248 | bytes 20979712 | tf_op jit(solution)/shard_map/etf,edf->etd/dot_general | solution.py:53
  236.5 7.1 fusion
  245.5 3.4 convolution_bitcast_fusion.1
  250.5 3.4 convolution_bitcast_fusion
  259.5 8.9 %multiply_reduce_fusion.1 = bf16[1024,1536]{1,0:T(8,128)(2,1)} fusion(f32[2,1024]{1,0:T(2,128)S(1)} %copy.79, bf16[2,1024,512]{1,2,0:T(8,128)(2,1)} %get-tuple-element.60, bf16[2,512,1536]{2,1,0:T(8,128)(2,1)} %constant_dynamic-update-slice_fusion), kind=kOutput, calls=%fused_computation.2 | convolution fusion | flops 3232235520 | bytes 8396800 | tf_op jit(solution)/shard_map/etf,efd->etd/dot_general | solution.py:53
  268.4 40.6 %reduce-scatter.5.cloned.1.call-done = bf16[128,1536]{1,0:T(8,128)(2,1)} async-done(((bf16[1024,1536]{1,0:T(8,128)(2,1)}), bf16[128,1536]{1,0:T(8,128)(2,1)}) %reduce-scatter.5.cloned.1.call-update) | async-done | bytes 393232 | tf_op jit(solution)/shard_map/reduce_scatter | solution.py:124
  319.5 3.2 fusion.21
  341.9 88.6 %all-reduce.7.cloned.1.call-done = (bf16[2,1536,256]{1,2,0:T(8,128)(2,1)}, bf16[2,1536,256]{1,2,0:T(8,128)(2,1)}, bf16[2,256,1536]{2,1,0:T(8,128)(2,1)}) async-done(((bf16[2,1536,256]{1,2,0:T(8,128)(2,1)}, bf16[2,1536,256]{1,2,0:T(8,128)(2,1)}, bf16[2,256,1536]{2,1,0:T(8,128)(2,1)}), (bf16[2,1536,256]{1,2,0:T(8,128)(2,1)}, bf16[2,1536,256]{1,2,0:T(8,128)(2,1)}, ...) | async-done | bytes 4718608 | tf_op jit(solution)/shard_map/psum | solution.py:131
  430.5 3.1 copy.95
  433.6 3.1 copy.96
  436.7 3.6 convert_element_type.191
  442.9 40.8 %psum.56 = f32[2,1536]{1,0:T(2,128)} all-reduce(f32[2,1536]{1,0:T(2,128)} %pad_maximum_fusion.15), channel_id=1, replica_groups=mesh['dp'=2,'expert'=8,'tensor'=2] {'dp','expert','tensor'}, use_global_device_ids=true, to_apply=%region_13.14 | all-reduce | flops 3072 | bytes 24576 | tf_op jit(solution)/shard_map/psum | solution.py:172
  486.4 24.1 %reduce-scatter.3.cloned.1.call-done = bf16[128,1536]{1,0:T(8,128)(2,1)} async-done(((bf16[1024,1536]{1,0:T(8,128)(2,1)}), bf16[128,1536]{1,0:T(8,128)(2,1)}) %reduce-scatter.3.cloned.1.call-update) | async-done | bytes 393232 | tf_op jit(solution)/shard_map/reduce_scatter | solution.py:125
  510.6 3.3 subtract_add_fusion
  513.9 216.3 %all-reduce.5.cloned.1.call-done = (bf16[1536,768]{1,0:T(8,128)(2,1)}, bf16[1536,256]{1,0:T(8,128)(2,1)}, bf16[1536,256]{1,0:T(8,128)(2,1)}, bf16[768,1536]{1,0:T(8,128)(2,1)}) async-done(((bf16[1536,768]{1,0:T(8,128)(2,1)}, bf16[1536,256]{1,0:T(8,128)(2,1)}, bf16[1536,256]{1,0:T(8,128)(2,1)}, bf16[768,1536]{1,0:T(8,128)(2,1)}), (bf16[1536,768]{1,0:T(8,128)(2,1)}, bf16[1536,256]{1,0:T(8,128)(2,1)}, ...) | async-done | bytes 6291472 | tf_op jit(solution)/shard_map/psum | solution.py:171
  736.6 2.8 convert_element_type.182
  (238 shorter events, 85.7 us)
Async XLA Ops:
  7.2 13.0 %copy-start = (bf16[768,1536]{1,0:T(8,128)(2,1)S(1)}, bf16[768,1536]{1,0:T(8,128)(2,1)}, u32[]{:S(2)}) copy-start(bf16[768,1536]{1,0:T(8,128)(2,1)} %param.23) | copy-start | bytes 7077892
  7.2 81.2 %all-gather.5.cloned.1.call-start = ((), (), s32[]{:S(2)}) async-start(), calls=%async_computation.3 | async-start | bytes 3538944 | tf_op jit(solution)/shard_map/all_gather | solution.py:109
  7.3 3.8 collective-permute-start
  10.2 9.1 %copy-start.42 = (pred[256,256]{0,1:T(8,128)(4,1)}, pred[256,256]{0,1:T(8,128)(4,1)S(1)}, u32[]{:S(2)}) copy-start(pred[256,256]{0,1:T(8,128)(4,1)S(1)} %compare_and_fusion) | copy-start | bytes 196612
  11.0 10.1 %copy-start.16 = (bf16[128,1536]{1,0:T(8,128)(2,1)}, bf16[128,1536]{1,0:T(8,128)(2,1)S(1)}, u32[]{:S(2)}) copy-start(bf16[128,1536]{1,0:T(8,128)(2,1)S(1)} %collective-permute-done) | copy-start | bytes 1179652
  21.1 2.4 collective-permute-start.1
  25.6 169.8 %all-gather.3.cloned.1.call-start = ((), (), s32[]{:S(2)}) async-start(), calls=%async_computation.2 | async-start | bytes 7667712 | tf_op jit(solution)/shard_map/all_gather | solution.py:17
  30.0 279.0 %reduce-scatter.5.cloned.1.call-start = ((), (), s32[]{:S(2)}) async-start(), calls=%async_computation.5 | async-start | bytes 3538944 | tf_op jit(solution)/shard_map/reduce_scatter | solution.py:124
  30.5 8.6 %collective-permute-start.4 = (bf16[2,256,1536]{2,1,0:T(8,128)(2,1)}, bf16[2,256,1536]{2,1,0:T(8,128)(2,1)}, u32[]{:S(2)}, u32[]{:S(2)}) collective-permute-start(bf16[2,256,1536]{2,1,0:T(8,128)(2,1)} %param.26), channel_id=1, source_target_pairs={{0,1},{1,0},{2,3},{3,2},{4,5},{5,4},{6,7},{7,6},{8,9},{9,8},{10,11... | collective-permute-start | bytes 4718600 | tf_op jit(solution)/shard_map/ppermute | solution.py:23
  33.3 8.5 %collective-permute-start.3 = (bf16[2,1536,256]{1,2,0:T(8,128)(2,1)}, bf16[2,1536,256]{1,2,0:T(8,128)(2,1)}, u32[]{:S(2)}, u32[]{:S(2)}) collective-permute-start(bf16[2,1536,256]{1,2,0:T(8,128)(2,1)} %copy.83), channel_id=1, source_target_pairs={{0,1},{1,0},{2,3},{3,2},{4,5},{5,4},{6,7},{7,6},{8,9},{9,8},{10,11... | collective-permute-start | bytes 4718600 | tf_op jit(solution)/shard_map/ppermute | solution.py:23
  36.2 60.7 %collective-permute-start.2 = (bf16[2,1536,256]{1,2,0:T(8,128)(2,1)}, bf16[2,1536,256]{1,2,0:T(8,128)(2,1)}, u32[]{:S(2)}, u32[]{:S(2)}) collective-permute-start(bf16[2,1536,256]{1,2,0:T(8,128)(2,1)} %copy.81), channel_id=1, source_target_pairs={{0,1},{1,0},{2,3},{3,2},{4,5},{5,4},{6,7},{7,6},{8,9},{9,8},{10,11... | collective-permute-start | bytes 4718600 | tf_op jit(solution)/shard_map/ppermute | solution.py:23
  202.7 11.6 %copy-start.1 = (f32[1024,1536]{1,0:T(8,128)}, f32[1024,1536]{1,0:T(8,128)S(1)}, u32[]{:S(2)}) copy-start(f32[1024,1536]{1,0:T(8,128)S(1)} %split.72) | copy-start | bytes 18874372
  202.7 11.7 %copy-start.12 = (bf16[2,1536,256]{1,2,0:T(8,128)(2,1)S(1)}, bf16[2,1536,256]{1,2,0:T(8,128)(2,1)}, u32[]{:S(2)}) copy-start(bf16[2,1536,256]{1,2,0:T(8,128)(2,1)} %copy.83) | copy-start | bytes 4718596
  236.2 194.3 %all-reduce.7.cloned.1.call-start = ((), (), s32[]{:S(2)}) async-start(), calls=%async_computation.7 | async-start | bytes 9437184 | tf_op jit(solution)/shard_map/psum | solution.py:131
  243.8 10.4 %collective-permute-start.9 = (bf16[2,256,1536]{2,1,0:T(8,128)(2,1)S(1)}, bf16[2,256,1536]{2,1,0:T(8,128)(2,1)S(1)}, u32[]{:S(2)}, u32[]{:S(2)}) collective-permute-start(bf16[2,256,1536]{2,1,0:T(8,128)(2,1)S(1)} %split.111), channel_id=1, source_target_pairs={{0,1},{1,0},{2,3},{3,2},{4,5},{5,4},{6,7},{7,6},{8,9},{9,8},{10,11... | collective-permute-start | bytes 4718600 | tf_op jit(solution)/shard_map/ppermute | solution.py:23
  249.1 6.7 collective-permute-start.7
  254.1 3.5 collective-permute-start.8
  259.2 251.4 %reduce-scatter.3.cloned.1.call-start = ((), (), s32[]{:S(2)}) async-start(), calls=%async_computation.4 | async-start | bytes 3538944 | tf_op jit(solution)/shard_map/reduce_scatter | solution.py:125
  268.4 40.7 %copy-start.53 = (f32[128]{0:T(128)S(1)}, f32[128]{0:T(128)}, u32[]{:S(2)}) copy-start(f32[128]{0:T(128)} %copy-done.52) | copy-start | bytes 1540
  268.4 42.5 %copy-start.55 = (f32[128]{0:T(128)S(1)}, f32[128]{0:T(128)}, u32[]{:S(2)}) copy-start(f32[128]{0:T(128)} %get-tuple-element.79) | copy-start | bytes 1540
  268.4 461.8 %all-reduce.5.cloned.1.call-start = ((), (), s32[]{:S(2)}) async-start(), calls=%async_computation.6 | async-start | bytes 12582912 | tf_op jit(solution)/shard_map/psum | solution.py:171
  312.3 1.8 collective-permute-start.5
  340.6 99.8 %collective-permute-start.6 = (f32[128,1536]{1,0:T(8,128)}, f32[128,1536]{1,0:T(8,128)}, u32[]{:S(2)}, u32[]{:S(2)}) collective-permute-start(f32[128,1536]{1,0:T(8,128)} %slice.53), channel_id=1, source_target_pairs={{0,1},{1,0},{2,3},{3,2},{4,5},{5,4},{6,7},{7,6},{8,9},{9,8},{10,11... | collective-permute-start | bytes 2359304 | tf_op jit(solution)/shard_map/ppermute | solution.py:23
  440.3 70.2 %copy-start.6 = (bf16[128,1536]{1,0:T(8,128)(2,1)S(1)}, bf16[128,1536]{1,0:T(8,128)(2,1)}, u32[]{:S(2)}) copy-start(bf16[128,1536]{1,0:T(8,128)(2,1)} %param.27) | copy-start | bytes 1179652
  (59 other events, 173.2 us)
Sparse Core Ops, SparseCore 0:
  25.7 62.6 all-gather.4
  91.2 104.1 all-gather.2
  236.3 72.6 reduce-scatter.4
  311.5 119.0 all-reduce.6
  435.0 75.5 reduce-scatter.2
  518.5 211.5 all-reduce.4
